TPU v7x, 32 devices: a whole 2x2x4 slice. The times are simulated.
32 devices in a mesh: row: 16 (over z, y, x), col: 2 (over core).
Axes of the slice: x: 2, y: 2, z: 4, core: 2. Of those that a mesh axis runs over, the one named last changes fastest.
Arguments:
- samples: bfloat16 [32768, 8192], P('row', 'col'), may hold values from -0.046875 to 0.046875
- targets: float32 [32768, 128], P('row'), may hold values from -6 to 6
- factor_inv: float32 [2, 4096, 4096], P('col', None, 'row'), may hold values from -1 to 1, as said below
Outputs:
- solution: float32 [8192, 128], P('col')
- residual: float32 [32768, 128], P('row')
Inputs may be any that keep to these rules, and one draw needn't show every extreme that they name: Each factor_inv[j] is lower triangular with a positive diagonal.
All inputs are finite; a program needn't handle non-finite values.
Results may differ from a plain program's by a relative error of at most 0.0039.
Values sent between devices are 32-bit elements; how exact they have to be, the bound alone decides.
A program may use at most 128 MiB of HBM per device.

v0:
```python
import jax
import jax.numpy as jnp
from jax import lax
from jax.sharding import PartitionSpec as P

ROUNDS = 3
ridge_weight = 0.5


def run_group(samples, residual, inverse, own_rows, offset, relaxation):
    solution = jnp.zeros((samples.shape[1], residual.shape[1]), jnp.float32)
    for sweep in range(ROUNDS):
        res16 = residual.astype(jnp.bfloat16)
        part_grad = jnp.einsum("rb,rk->bk", samples, res16, preferred_element_type=jnp.float32)
        own_solution = lax.dynamic_slice_in_dim(solution, offset, own_rows, 0)
        grad_own = (
            lax.psum_scatter(part_grad, "row", scatter_dimension=0, tiled=True)
            - ridge_weight * own_solution
        )
        term = jnp.dot(inverse, grad_own, precision=lax.Precision.HIGHEST)
        image = lax.psum(term, "row")
        update_own = jnp.einsum("bc,bk->ck", inverse, image, precision=lax.Precision.HIGHEST)
        update = lax.all_gather(update_own, "row", axis=0, tiled=True)
        solution = solution + relaxation * update
        change = jnp.dot(samples, update.astype(jnp.bfloat16), preferred_element_type=jnp.float32)
        residual = residual - relaxation * lax.psum(change, "col")
    return (solution, residual)


def per_device(samples, targets, factor_inv):
    inverse = factor_inv[0]
    own_rows = inverse.shape[1]
    offset = lax.axis_index("row") * own_rows
    relaxation = 1.0 / lax.axis_size("col")
    solution, residual = run_group(samples, targets, inverse, own_rows, offset, relaxation)
    return (solution, residual)


def solution(mesh):
    in_specs = (P("row", "col"), P("row", None), P("col", None, "row"))
    out_specs = (P("col", None), P("row", None))
    return jax.shard_map(
        per_device, mesh=mesh, in_specs=in_specs, out_specs=out_specs, check_vma=False
    )
```

profile of v0, /device:TPU:0, one launch (start us, length us, event | category | flops | bytes accessed | tf_op | source)
XLA Modules:
  0.0 985.5 jit_solution(3133331421541427131)
XLA Ops:
  7.2 0.0 reduce-scatter.4.cloned.1.call-start
  7.2 11.9 %fusion.23 = f32[4096,128]{1,0:T(8,128)} fusion(bf16[2048,4096]{1,0:T(8,128)(2,1)} %param.3, f32[2048,128]{1,0:T(8,128)} %param.4), kind=kOutput, calls=%fused_computation.31 | convolution fusion | flops 2147745792 | bytes 19922944 | tf_op jit(solution)/shard_map/rb,rk->bk/dot_general | solution.py:14
  19.1 0.0 reduce-scatter.4.cloned.1.call-update
  19.1 0.0 all-reduce.7.cloned.1.call-start
  19.2 83.5 %reduce-scatter.4.cloned.1.call-done = f32[256,128]{1,0:T(8,128)} async-done(((f32[4096,128]{1,0:T(8,128)}), f32[256,128]{1,0:T(8,128)}) %reduce-scatter.4.cloned.1.call-update) | async-done | bytes 131088 | tf_op jit(solution)/shard_map/reduce_scatter | solution.py:17
  102.7 8.1 convolution_bitcast_fusion.4
  110.7 0.0 all-reduce.7.cloned.1.call-update
  110.8 0.0 all-gather.4.cloned.1.call-start
  110.8 123.0 %all-reduce.7.cloned.1.call-done = f32[4096,128]{0,1:T(8,128)} async-done(((f32[4096,128]{0,1:T(8,128)}), f32[4096,128]{0,1:T(8,128)}) %all-reduce.7.cloned.1.call-update) | async-done | bytes 2097168 | tf_op jit(solution)/shard_map/psum | solution.py:21
  233.9 5.6 fusion.9
  239.4 0.0 all-gather.4.cloned.1.call-update
  239.5 0.0 copy-start.4
  239.5 0.5 all-reduce.9.cloned.1.call-start
  240.0 60.7 %all-gather.4.cloned.1.call-done = f32[4096,128]{0,1:T(8,128)} async-done(((f32[256,128]{0,1:T(8,128)}), f32[4096,128]{0,1:T(8,128)}) %all-gather.4.cloned.1.call-update) | async-done | bytes 2097168 | tf_op jit(solution)/shard_map/all_gather | solution.py:23
  300.7 13.0 %convolution_bitcast_fusion.7 = f32[2048,128]{0,1:T(8,128)} fusion(bf16[2048,4096]{1,0:T(8,128)(2,1)} %param.3, f32[4096,128]{0,1:T(8,128)} %all-gather.4.cloned.1.call-done), kind=kOutput, calls=%fused_computation.16 | convolution fusion | flops 2148007936 | bytes 19922944 | tf_op jit(solution)/shard_map/dot_general | solution.py:25
  313.7 0.0 all-reduce.9.cloned.1.call-update
  313.8 0.0 reduce-scatter.6.cloned.1.call-start
  313.8 0.0 copy-done.4
  313.8 0.3 copy.5
  314.2 17.5 %all-reduce.9.cloned.1.call-done = f32[2048,128]{0,1:T(8,128)} async-done(((f32[2048,128]{0,1:T(8,128)}), f32[2048,128]{0,1:T(8,128)}) %all-reduce.9.cloned.1.call-update) | async-done | bytes 1048592 | tf_op jit(solution)/shard_map/psum | solution.py:26
  331.7 9.8 convolution_bitcast_fusion.1
  341.5 0.0 copy-start
  341.5 0.0 reduce-scatter.6.cloned.1.call-update
  341.5 0.0 all-reduce.11.cloned.1.call-start
  341.6 1.5 copy-done
  343.1 1.5 broadcast_multiply_fusion
  344.6 78.9 %reduce-scatter.6.cloned.1.call-done = f32[256,128]{0,1:T(8,128)} async-done(((f32[4096,128]{0,1:T(8,128)}), f32[256,128]{0,1:T(8,128)}) %reduce-scatter.6.cloned.1.call-update) | async-done | bytes 131088 | tf_op jit(solution)/shard_map/reduce_scatter | solution.py:17
  423.5 7.9 convolution_bitcast_fusion.3
  431.4 0.0 all-reduce.11.cloned.1.call-update
  431.4 0.2 all-gather.6.cloned.1.call-start
  431.6 122.8 %all-reduce.11.cloned.1.call-done = f32[4096,128]{0,1:T(8,128)} async-done(((f32[4096,128]{0,1:T(8,128)}), f32[4096,128]{0,1:T(8,128)}) %all-reduce.11.cloned.1.call-update) | async-done | bytes 2097168 | tf_op jit(solution)/shard_map/psum | solution.py:21
  554.5 5.6 fusion.12
  560.0 0.0 all-gather.6.cloned.1.call-update
  560.1 0.0 all-reduce.13.cloned.1.call-start
  560.1 61.2 %all-gather.6.cloned.1.call-done = f32[4096,128]{0,1:T(8,128)} async-done(((f32[256,128]{0,1:T(8,128)}), f32[4096,128]{0,1:T(8,128)}) %all-gather.6.cloned.1.call-update) | async-done | bytes 2097168 | tf_op jit(solution)/shard_map/all_gather | solution.py:23
  621.3 13.0 %convolution_bitcast_fusion.6 = f32[2048,128]{0,1:T(8,128)} fusion(bf16[2048,4096]{1,0:T(8,128)(2,1)} %param.3, f32[4096,128]{0,1:T(8,128)} %all-gather.6.cloned.1.call-done), kind=kOutput, calls=%fused_computation.15 | convolution fusion | flops 2148007936 | bytes 19922944 | tf_op jit(solution)/shard_map/dot_general | solution.py:25
  634.3 0.0 all-reduce.13.cloned.1.call-update
  634.4 0.0 reduce-scatter.8.cloned.1.call-start
  634.4 17.9 %all-reduce.13.cloned.1.call-done = f32[2048,128]{0,1:T(8,128)} async-done(((f32[2048,128]{0,1:T(8,128)}), f32[2048,128]{0,1:T(8,128)}) %all-reduce.13.cloned.1.call-update) | async-done | bytes 1048592 | tf_op jit(solution)/shard_map/psum | solution.py:26
  652.3 10.2 %convolution_bitcast_fusion = f32[4096,128]{0,1:T(8,128)} fusion(bf16[2048,4096]{1,0:T(8,128)(2,1)} %param.3, f32[2048,128]{0,1:T(8,128)} %all-reduce.13.cloned.1.call-done, f32[2048,128]{0,1:T(8,128)S(1)} %copy.5, f32[2048,128]{0,1:T(8,128)} %all-reduce.9.cloned.1.call-done), kind=kOutput, calls=%fused_computation | convolution fusion | flops 2148794368 | bytes 22020096 | tf_op jit(solution)/shard_map/rb,rk->bk/dot_general | solution.py:14
  662.5 0.0 reduce-scatter.8.cloned.1.call-update
  662.5 0.3 all-reduce.15.cloned.1.call-start
  662.8 3.2 multiply_add_fusion.1
  665.9 78.6 %reduce-scatter.8.cloned.1.call-done = f32[256,128]{0,1:T(8,128)} async-done(((f32[4096,128]{0,1:T(8,128)}), f32[256,128]{0,1:T(8,128)}) %reduce-scatter.8.cloned.1.call-update) | async-done | bytes 131088 | tf_op jit(solution)/shard_map/reduce_scatter | solution.py:17
  744.5 7.9 convolution_bitcast_fusion.2
  752.5 0.0 all-reduce.15.cloned.1.call-update
  752.5 0.0 all-gather.8.cloned.1.call-start
  752.6 122.8 %all-reduce.15.cloned.1.call-done = f32[4096,128]{0,1:T(8,128)} async-done(((f32[4096,128]{0,1:T(8,128)}), f32[4096,128]{0,1:T(8,128)}) %all-reduce.15.cloned.1.call-update) | async-done | bytes 2097168 | tf_op jit(solution)/shard_map/psum | solution.py:21
  875.4 5.6 fusion.15
  881.0 0.0 all-gather.8.cloned.1.call-update
  881.0 0.0 all-reduce.17.cloned.1.call-start
  881.0 61.2 %all-gather.8.cloned.1.call-done = f32[4096,128]{0,1:T(8,128)} async-done(((f32[256,128]{0,1:T(8,128)}), f32[4096,128]{0,1:T(8,128)}) %all-gather.8.cloned.1.call-update) | async-done | bytes 2097168 | tf_op jit(solution)/shard_map/all_gather | solution.py:23
  942.2 0.0 copy-start.2
  942.2 13.2 %convolution_bitcast_fusion.5 = f32[2048,128]{0,1:T(8,128)} fusion(bf16[2048,4096]{1,0:T(8,128)(2,1)} %param.3, f32[4096,128]{0,1:T(8,128)} %all-gather.8.cloned.1.call-done), kind=kOutput, calls=%fused_computation.14 | convolution fusion | flops 2148007936 | bytes 19922944 | tf_op jit(solution)/shard_map/dot_general | solution.py:25
  955.4 0.0 all-reduce.17.cloned.1.call-update
  955.4 0.0 copy-done.2
  955.4 3.1 multiply_add_fusion
  958.6 0.0 copy-start.1
  958.6 3.3 copy.6
  961.9 11.5 %all-reduce.17.cloned.1.call-done = f32[2048,128]{0,1:T(8,128)} async-done(((f32[2048,128]{0,1:T(8,128)}), f32[2048,128]{0,1:T(8,128)}) %all-reduce.17.cloned.1.call-update) | async-done | bytes 1048592 | tf_op jit(solution)/shard_map/psum | solution.py:26
  973.4 0.0 copy-done.1
  973.4 0.0 copy-done.3
  973.4 2.5 multiply_subtract_fusion
  975.9 2.5 copy.7
  (1 shorter events, 0.0 us)
Async XLA Ops:
  7.2 95.5 %reduce-scatter.4.cloned.1.call-start = ((), (), s32[]{:S(2)}) async-start(), calls=%async_computation.3 | async-start | bytes 2228224 | tf_op jit(solution)/shard_map/reduce_scatter | solution.py:17
  19.1 214.7 %all-reduce.7.cloned.1.call-start = ((), (), s32[]{:S(2)}) async-start(), calls=%async_computation.4 | async-start | bytes 4194304 | tf_op jit(solution)/shard_map/psum | solution.py:21
  110.8 190.0 %all-gather.4.cloned.1.call-start = ((), (), s32[]{:S(2)}) async-start(), calls=%async_computation.5 | async-start | bytes 2228224 | tf_op jit(solution)/shard_map/all_gather | solution.py:23
  239.5 74.4 %copy-start.4 = (f32[2048,128]{1,0:T(8,128)S(1)}, f32[2048,128]{1,0:T(8,128)}, u32[]{:S(2)}) copy-start(f32[2048,128]{1,0:T(8,128)} %param.4) | copy-start | bytes 3145732
  239.5 92.2 %all-reduce.9.cloned.1.call-start = ((), (), s32[]{:S(2)}) async-start(), calls=%async_computation.6 | async-start | bytes 2097152 | tf_op jit(solution)/shard_map/psum | solution.py:26
  313.8 109.7 %reduce-scatter.6.cloned.1.call-start = ((), (), s32[]{:S(2)}) async-start(), calls=%async_computation.7 | async-start | bytes 2228224 | tf_op jit(solution)/shard_map/reduce_scatter | solution.py:17
  341.5 1.6 copy-start
  341.5 213.0 %all-reduce.11.cloned.1.call-start = ((), (), s32[]{:S(2)}) async-start(), calls=%async_computation.8 | async-start | bytes 4194304 | tf_op jit(solution)/shard_map/psum | solution.py:21
  431.4 189.9 %all-gather.6.cloned.1.call-start = ((), (), s32[]{:S(2)}) async-start(), calls=%async_computation.9 | async-start | bytes 2228224 | tf_op jit(solution)/shard_map/all_gather | solution.py:23
  560.1 92.3 %all-reduce.13.cloned.1.call-start = ((), (), s32[]{:S(2)}) async-start(), calls=%async_computation.10 | async-start | bytes 2097152 | tf_op jit(solution)/shard_map/psum | solution.py:26
  634.4 110.2 %reduce-scatter.8.cloned.1.call-start = ((), (), s32[]{:S(2)}) async-start(), calls=%async_computation.11 | async-start | bytes 2228224 | tf_op jit(solution)/shard_map/reduce_scatter | solution.py:17
  662.5 212.9 %all-reduce.15.cloned.1.call-start = ((), (), s32[]{:S(2)}) async-start(), calls=%async_computation.12 | async-start | bytes 4194304 | tf_op jit(solution)/shard_map/psum | solution.py:21
  752.5 189.7 %all-gather.8.cloned.1.call-start = ((), (), s32[]{:S(2)}) async-start(), calls=%async_computation.13 | async-start | bytes 2228224 | tf_op jit(solution)/shard_map/all_gather | solution.py:23
  881.0 92.4 %all-reduce.17.cloned.1.call-start = ((), (), s32[]{:S(2)}) async-start(), calls=%async_computation.14 | async-start | bytes 2097152 | tf_op jit(solution)/shard_map/psum | solution.py:26
  942.2 13.2 %copy-start.2 = (f32[4096,128]{0,1:T(8,128)S(1)}, f32[4096,128]{0,1:T(8,128)}, u32[]{:S(2)}) copy-start(f32[4096,128]{0,1:T(8,128)} %multiply_add_fusion.1) | copy-start | bytes 6291460
  958.6 14.8 %copy-start.1 = (f32[2048,128]{0,1:T(8,128)S(1)}, f32[2048,128]{0,1:T(8,128)}, u32[]{:S(2)}) copy-start(f32[2048,128]{0,1:T(8,128)} %all-reduce.9.cloned.1.call-done) | copy-start | bytes 3145732
  958.6 14.8 %copy-start.3 = (f32[2048,128]{0,1:T(8,128)S(1)}, f32[2048,128]{0,1:T(8,128)}, u32[]{:S(2)}) copy-start(f32[2048,128]{0,1:T(8,128)} %all-reduce.13.cloned.1.call-done) | copy-start | bytes 3145732
Sparse Core Ops, SparseCore 0:
  19.3 83.3 reduce-scatter.3
  110.9 122.9 all-reduce.6
  239.6 61.0 all-gather.3
  313.9 17.7 all-reduce.8
  341.6 81.7 reduce-scatter.5
  431.5 122.8 all-reduce.10
  560.2 61.0 all-gather.5
  634.5 17.7 all-reduce.12
  662.6 81.8 reduce-scatter.7
  752.6 122.7 all-reduce.14
  881.1 61.0 all-gather.7
  955.6 17.7 all-reduce.16
where the time goes:
time: 994 us; the launch traced here: 986 us
  waiting for transfers between devices  840 us (85%)
  matrix products  112 us (11%)
  between operations  14.5 us (1%)
  other arithmetic  10.3 us (1%)
    psum x3, waiting for transfers between devices, run_group(): image = lax.psum(term, 'row')  369 us
    reduce_scatter x3, waiting for transfers between devices, run_group(): lax.psum_scatter(part_grad, 'row', scatter_dimension=0, tiled=True)  241 us
    all_gather x3, waiting for transfers between devices, run_group(): update = lax.all_gather(update_own, 'row', axis=0, tiled=True)  183 us
    psum x3, waiting for transfers between devices, run_group(): residual = residual - relaxation * lax.psum(change, 'col')  46.9 us
    dot_general x3, matrix products, run_group(): jnp.dot(samples, update.astype(jnp.bfloat16), preferred_element_type=jnp....  39.2 us
    dot_general x3, matrix products, run_group(): jnp.einsum('rb,rk->bk', samples, res16, preferred_element_type=jnp.float32)  31.9 us
    dot_general x3, matrix products, run_group(): term = jnp.dot(inverse, grad_own, precision=lax.Precision.HIGHEST)  23.9 us
  transfers between devices with their start and end apart: 12, of which 12 were waited for; matrix products, arithmetic and copies ran while one was open for 1% of the time, Pallas kernels for 0%

commit v1 on v0

--- a/solution.py
+++ b/solution.py
@@ -20,7 +20,26 @@
         term = jnp.dot(inverse, grad_own, precision=lax.Precision.HIGHEST)
         image = lax.psum(term, "row")
         update_own = jnp.einsum("bc,bk->ck", inverse, image, precision=lax.Precision.HIGHEST)
-        update = lax.all_gather(update_own, "row", axis=0, tiled=True)
+        size, index, width = (lax.axis_size("row"), lax.axis_index("row"), update_own.shape[0])
+        right = [(i, (i + 1) % size) for i in range(size)]
+        left = [(i, (i - 1) % size) for i in range(size)]
+        out = jnp.zeros(
+            (*update_own.shape[:0], size * width, *update_own.shape[0 + 1 :]), update_own.dtype
+        )
+        out = lax.dynamic_update_slice_in_dim(out, update_own, index * width, axis=0)
+        from_left = from_right = update_own
+        middle = size // 2
+        for step in range(1, middle + 1):
+            from_left = lax.ppermute(from_left, "row", right)
+            out = lax.dynamic_update_slice_in_dim(
+                out, from_left, (index - step) % size * width, axis=0
+            )
+            if step < size - middle:
+                from_right = lax.ppermute(from_right, "row", left)
+                out = lax.dynamic_update_slice_in_dim(
+                    out, from_right, (index + step) % size * width, axis=0
+                )
+        update = out
         solution = solution + relaxation * update
         change = jnp.dot(samples, update.astype(jnp.bfloat16), preferred_element_type=jnp.float32)
         residual = residual - relaxation * lax.psum(change, "col")

time: 994 us -> 1040 us (1.046)
  starting transfers between devices: 1.35 us -> 124 us
  waiting for transfers between devices: 840 us -> 732 us
  local copies, waits for them, and re-layouts: 7.7 us -> 34.4 us
    all_gather x3 -> x0, waiting for transfers between devices: 183 us -> none  [run_group(): update = lax.all_gather(update_own, 'row', axis=0, tiled=True)]
    ppermute x0 -> x45, starting transfers between devices: none -> 123 us  [the longest x21 117 us: run_group(): from_right = lax.ppermute(from_right, 'row', left)]
    ppermute x0 -> x45, waiting for transfers between devices: none -> 78.2 us  [the longest x24 77.8 us: run_group(): from_left = lax.ppermute(from_left, 'row', right)]
    ppermute x0 -> x45, local copies, waits for them, and re-layouts: none -> 18.4 us  [the longest x24 16.6 us: run_group(): from_left = lax.ppermute(from_left, 'row', right)]
    dynamic_update_slice x0 -> x48, local copies, waits for them, and re-layouts: none -> 11.2 us  [the longest x24 5.63 us: run_group(): lax.dynamic_update_slice_in_dim(out, from_left, (index - step) % size * w...]
  transfers between devices with their start and end apart: 12 -> 54, of which waited for: 12 -> 34; matrix products, arithmetic and copies ran while one was open for 1% -> 4% of each run, Pallas kernels for 0% -> 0%
where the time goes in v1:
time: 1040 us; the launch traced here: 1030 us
  waiting for transfers between devices  732 us (70%)
  starting transfers between devices  124 us (12%)
  matrix products  117 us (11%)
  local copies, waits for them, and re-layouts  34.4 us (3%)
  between operations  15.2 us (1%)
    psum x3, waiting for transfers between devices, run_group(): image = lax.psum(term, 'row')  369 us
    reduce_scatter x3, waiting for transfers between devices, run_group(): lax.psum_scatter(part_grad, 'row', scatter_dimension=0, tiled=True)  243 us
    ppermute x21, starting transfers between devices, run_group(): from_right = lax.ppermute(from_right, 'row', left)  117 us
    ppermute x24, waiting for transfers between devices, run_group(): from_left = lax.ppermute(from_left, 'row', right)  77.8 us
    psum x3, waiting for transfers between devices, run_group(): residual = residual - relaxation * lax.psum(change, 'col')  41.9 us
    dot_general x3, matrix products, run_group(): jnp.einsum('rb,rk->bk', samples, res16, preferred_element_type=jnp.float32)  40.4 us
    dot_general x3, matrix products, run_group(): jnp.dot(samples, update.astype(jnp.bfloat16), preferred_element_type=jnp....  37.8 us
    dot_general x3, matrix products, run_group(): term = jnp.dot(inverse, grad_own, precision=lax.Precision.HIGHEST)  24.3 us
  transfers between devices with their start and end apart: 54, of which 34 were waited for; matrix products, arithmetic and copies ran while one was open for 4% of the time, Pallas kernels for 0%

profile of v1, /device:TPU:0, one launch (start us, length us, event | category | flops | bytes accessed | tf_op | source)
XLA Modules:
  0.0 1032.5 jit_solution(9445597813002956916)
XLA Ops:
  7.2 11.9 %fusion.23 = f32[4096,128]{1,0:T(8,128)} fusion(bf16[2048,4096]{1,0:T(8,128)(2,1)} %param.3, f32[2048,128]{1,0:T(8,128)} %param.4), kind=kOutput, calls=%fused_computation.31 | convolution fusion | flops 2147745792 | bytes 19922944 | tf_op jit(solution)/shard_map/rb,rk->bk/dot_general | solution.py:14
  19.2 83.5 %reduce-scatter.4.cloned.1.call-done = f32[256,128]{1,0:T(8,128)} async-done(((f32[4096,128]{1,0:T(8,128)}), f32[256,128]{1,0:T(8,128)}) %reduce-scatter.4.cloned.1.call-update) | async-done | bytes 131088 | tf_op jit(solution)/shard_map/reduce_scatter | solution.py:17
  102.7 8.1 convolution_bitcast_fusion.4
  110.8 123.0 %all-reduce.7.cloned.1.call-done = f32[4096,128]{0,1:T(8,128)} async-done(((f32[4096,128]{0,1:T(8,128)}), f32[4096,128]{0,1:T(8,128)}) %all-reduce.7.cloned.1.call-update) | async-done | bytes 2097168 | tf_op jit(solution)/shard_map/psum | solution.py:21
  233.9 4.9 fusion.9
  240.4 4.2 collective-permute-start.1
  244.8 3.2 collective-permute-done
  248.3 6.0 collective-permute-start.3
  254.3 2.5 collective-permute-done.2
  257.1 6.0 collective-permute-start.5
  263.1 2.5 collective-permute-done.4
  265.9 6.0 collective-permute-start.7
  272.0 2.4 collective-permute-done.6
  274.7 6.1 collective-permute-start.9
  280.8 2.4 collective-permute-done.8
  283.5 6.1 collective-permute-start.11
  289.6 2.5 collective-permute-done.10
  292.7 6.2 collective-permute-start.13
  298.9 3.2 collective-permute-done.12
  302.4 8.4 collective-permute-done.14
  310.9 12.4 %convolution_bitcast_fusion.7 = f32[2048,128]{0,1:T(8,128)} fusion(bf16[2048,4096]{1,0:T(8,128)(2,1)} %param.3, f32[4096,128]{1,0:T(8,128)S(1)} %constant_dynamic-update-slice_fusion.32), kind=kOutput, calls=%fused_computation.16 | convolution fusion | flops 2148007936 | bytes 19922944 | tf_op jit(solution)/shard_map/dot_general | solution.py:44
  325.0 14.0 %all-reduce.9.cloned.1.call-done = f32[2048,128]{0,1:T(8,128)} async-done(((f32[2048,128]{0,1:T(8,128)}), f32[2048,128]{0,1:T(8,128)}) %all-reduce.9.cloned.1.call-update) | async-done | bytes 1048592 | tf_op jit(solution)/shard_map/psum | solution.py:45
  339.0 14.0 %convolution_bitcast_fusion.1 = f32[4096,128]{1,0:T(8,128)} fusion(bf16[2048,4096]{1,0:T(8,128)(2,1)} %param.3, f32[2048,128]{0,1:T(8,128)S(1)} %copy.21, f32[2048,128]{0,1:T(8,128)} %all-reduce.9.cloned.1.call-done), kind=kOutput, calls=%fused_computation.1 | convolution fusion | flops 2148270080 | bytes 20971520 | tf_op jit(solution)/shard_map/rb,rk->bk/dot_general | solution.py:14
  354.6 80.4 %reduce-scatter.6.cloned.1.call-done = f32[256,128]{1,0:T(8,128)} async-done(((f32[4096,128]{1,0:T(8,128)}), f32[256,128]{1,0:T(8,128)}) %reduce-scatter.6.cloned.1.call-update) | async-done | bytes 131088 | tf_op jit(solution)/shard_map/reduce_scatter | solution.py:17
  435.0 8.1 convolution_bitcast_fusion.3
  443.3 123.1 %all-reduce.11.cloned.1.call-done = f32[4096,128]{0,1:T(8,128)} async-done(((f32[4096,128]{0,1:T(8,128)}), f32[4096,128]{0,1:T(8,128)}) %all-reduce.11.cloned.1.call-update) | async-done | bytes 2097168 | tf_op jit(solution)/shard_map/psum | solution.py:21
  566.4 4.9 fusion.12
  572.9 4.2 collective-permute-start.16
  582.5 5.7 collective-permute-start.18
  588.8 1.8 collective-permute-done.17
  592.5 5.7 collective-permute-start.20
  602.4 5.7 collective-permute-start.22
  612.3 5.7 collective-permute-start.24
  622.3 5.7 collective-permute-start.26
  628.6 1.9 collective-permute-done.25
  632.3 5.7 collective-permute-start.28
  643.0 7.4 collective-permute-done.29
  652.1 13.0 %convolution_bitcast_fusion.6 = f32[2048,128]{0,1:T(8,128)} fusion(bf16[2048,4096]{1,0:T(8,128)(2,1)} %param.3, f32[4096,128]{1,0:T(8,128)} %constant_dynamic-update-slice_fusion.16), kind=kOutput, calls=%fused_computation.15 | convolution fusion | flops 2148007936 | bytes 19922944 | tf_op jit(solution)/shard_map/dot_general | solution.py:44
  665.4 15.4 %all-reduce.13.cloned.1.call-done = f32[2048,128]{0,1:T(8,128)} async-done(((f32[2048,128]{0,1:T(8,128)}), f32[2048,128]{0,1:T(8,128)}) %all-reduce.13.cloned.1.call-update) | async-done | bytes 1048592 | tf_op jit(solution)/shard_map/psum | solution.py:45
  680.8 14.4 %convolution_bitcast_fusion = f32[4096,128]{1,0:T(8,128)} fusion(bf16[2048,4096]{1,0:T(8,128)(2,1)} %param.3, f32[2048,128]{0,1:T(8,128)} %all-reduce.13.cloned.1.call-done, f32[2048,128]{0,1:T(8,128)S(1)} %copy.21, f32[2048,128]{0,1:T(8,128)} %all-reduce.9.cloned.1.call-done), kind=kOutput, calls=%fused_computation | convolution fusion | flops 2148794368 | bytes 22020096 | tf_op jit(solution)/shard_map/rb,rk->bk/dot_general | solution.py:14
  695.3 3.1 multiply_add_fusion.1
  698.4 78.7 %reduce-scatter.8.cloned.1.call-done = f32[256,128]{1,0:T(8,128)} async-done(((f32[4096,128]{1,0:T(8,128)}), f32[256,128]{1,0:T(8,128)}) %reduce-scatter.8.cloned.1.call-update) | async-done | bytes 131088 | tf_op jit(solution)/shard_map/reduce_scatter | solution.py:17
  777.1 8.2 convolution_bitcast_fusion.2
  785.6 123.0 %all-reduce.15.cloned.1.call-done = f32[4096,128]{0,1:T(8,128)} async-done(((f32[4096,128]{0,1:T(8,128)}), f32[4096,128]{0,1:T(8,128)}) %all-reduce.15.cloned.1.call-update) | async-done | bytes 2097168 | tf_op jit(solution)/shard_map/psum | solution.py:21
  908.6 4.9 fusion.15
  915.1 4.2 collective-permute-start.31
  919.5 3.3 collective-permute-done.30
  924.0 5.7 collective-permute-start.33
  929.7 3.2 collective-permute-done.32
  934.1 5.7 collective-permute-start.35
  939.7 3.1 collective-permute-done.34
  944.0 5.7 collective-permute-start.37
  949.7 3.1 collective-permute-done.36
  954.0 5.7 collective-permute-start.39
  959.7 3.2 collective-permute-done.38
  964.0 5.7 collective-permute-start.41
  969.7 3.1 collective-permute-done.40
  974.0 5.7 collective-permute-start.43
  979.7 3.4 collective-permute-done.42
  984.3 8.7 collective-permute-done.44
  994.0 12.4 %convolution_bitcast_fusion.5 = f32[2048,128]{0,1:T(8,128)} fusion(bf16[2048,4096]{1,0:T(8,128)(2,1)} %param.3, f32[4096,128]{1,0:T(8,128)S(1)} %constant_dynamic-update-slice_fusion), kind=kOutput, calls=%fused_computation.14 | convolution fusion | flops 2148007936 | bytes 19922944 | tf_op jit(solution)/shard_map/dot_general | solution.py:44
  1006.5 3.1 multiply_add_fusion
  1009.6 12.5 %all-reduce.17.cloned.1.call-done = f32[2048,128]{0,1:T(8,128)} async-done(((f32[2048,128]{0,1:T(8,128)}), f32[2048,128]{0,1:T(8,128)}) %all-reduce.17.cloned.1.call-update) | async-done | bytes 1048592 | tf_op jit(solution)/shard_map/psum | solution.py:45
  1022.1 2.2 multiply_subtract_fusion
  (170 shorter events, 51.8 us)
Async XLA Ops:
  7.2 95.5 %reduce-scatter.4.cloned.1.call-start = ((), (), s32[]{:S(2)}) async-start(), calls=%async_computation.3 | async-start | bytes 2228224 | tf_op jit(solution)/shard_map/reduce_scatter | solution.py:17
  19.2 214.7 %all-reduce.7.cloned.1.call-start = ((), (), s32[]{:S(2)}) async-start(), calls=%async_computation.4 | async-start | bytes 4194304 | tf_op jit(solution)/shard_map/psum | solution.py:21
  110.8 228.2 %all-reduce.9.cloned.1.call-start = ((), (), s32[]{:S(2)}) async-start(), calls=%async_computation.5 | async-start | bytes 2097152 | tf_op jit(solution)/shard_map/psum | solution.py:45
  238.8 9.2 collective-permute-start
  240.4 7.8 collective-permute-start.1
  248.1 8.7 collective-permute-start.2
  248.3 8.7 collective-permute-start.3
  256.9 8.7 collective-permute-start.4
  257.1 8.7 collective-permute-start.5
  265.7 8.7 collective-permute-start.6
  265.9 8.7 collective-permute-start.7
  274.5 8.7 collective-permute-start.8
  274.7 8.7 collective-permute-start.9
  283.3 8.8 collective-permute-start.10
  283.5 9.1 collective-permute-start.11
  292.2 9.9 collective-permute-start.12
  292.7 9.6 collective-permute-start.13
  302.2 8.6 collective-permute-start.14
  323.3 111.6 %reduce-scatter.6.cloned.1.call-start = ((), (), s32[]{:S(2)}) async-start(), calls=%async_computation.6 | async-start | bytes 2228224 | tf_op jit(solution)/shard_map/reduce_scatter | solution.py:17
  353.0 213.4 %all-reduce.11.cloned.1.call-start = ((), (), s32[]{:S(2)}) async-start(), calls=%async_computation.7 | async-start | bytes 4194304 | tf_op jit(solution)/shard_map/psum | solution.py:21
  443.1 237.7 %all-reduce.13.cloned.1.call-start = ((), (), s32[]{:S(2)}) async-start(), calls=%async_computation.8 | async-start | bytes 2097152 | tf_op jit(solution)/shard_map/psum | solution.py:45
  571.3 9.3 collective-permute-start.15
  572.9 9.4 collective-permute-start.16
  581.6 9.0 collective-permute-start.17
  582.5 9.9 collective-permute-start.18
  591.6 8.9 collective-permute-start.19
  592.5 9.8 collective-permute-start.20
  601.6 8.9 collective-permute-start.21
  602.4 9.9 collective-permute-start.22
  611.5 9.0 collective-permute-start.23
  612.3 9.9 collective-permute-start.24
  621.5 9.0 collective-permute-start.25
  622.3 9.9 collective-permute-start.26
  631.5 9.0 collective-permute-start.27
  632.3 9.9 collective-permute-start.28
  641.5 8.9 collective-permute-start.29
  665.2 112.0 %reduce-scatter.8.cloned.1.call-start = ((), (), s32[]{:S(2)}) async-start(), calls=%async_computation.9 | async-start | bytes 2228224 | tf_op jit(solution)/shard_map/reduce_scatter | solution.py:17
  695.2 213.4 %all-reduce.15.cloned.1.call-start = ((), (), s32[]{:S(2)}) async-start(), calls=%async_computation.10 | async-start | bytes 4194304 | tf_op jit(solution)/shard_map/psum | solution.py:21
  785.3 236.8 %all-reduce.17.cloned.1.call-start = ((), (), s32[]{:S(2)}) async-start(), calls=%async_computation.11 | async-start | bytes 2097152 | tf_op jit(solution)/shard_map/psum | solution.py:45
  913.5 9.3 collective-permute-start.30
  915.1 8.8 collective-permute-start.31
  923.8 9.0 collective-permute-start.32
  924.0 9.9 collective-permute-start.33
  933.9 8.9 collective-permute-start.34
  934.1 9.8 collective-permute-start.35
  943.8 9.0 collective-permute-start.36
  944.0 9.9 collective-permute-start.37
  953.8 9.0 collective-permute-start.38
  954.0 9.9 collective-permute-start.39
  963.8 9.0 collective-permute-start.40
  964.0 9.9 collective-permute-start.41
  973.8 9.3 collective-permute-start.42
  974.0 10.2 collective-permute-start.43
  984.1 8.9 collective-permute-start.44
Sparse Core Ops, SparseCore 0:
  19.3 83.3 reduce-scatter.3
  110.9 122.9 all-reduce.6
  323.5 15.4 all-reduce.8
  353.2 81.7 reduce-scatter.5
  443.2 123.1 all-reduce.10
  665.3 15.4 all-reduce.12
  695.3 81.7 reduce-scatter.7
  785.4 123.1 all-reduce.14
  1006.6 15.4 all-reduce.16
